TPU v7x, 256 devices: a whole 4x4x8 slice. The times are simulated.
256 devices in a mesh: row: 16 (over y_lo, z), vec: 16 (over y_hi, x, core).
Axes of the slice: x: 4, y: 4 (y_hi: 2, y_lo: 2; y = y_hi * 2 + y_lo), z: 8, core: 2. Of those that a mesh axis runs over, the one named last changes fastest.
Arguments:
- vectors: float32 [16384, 6144], P('row', 'vec'), may hold values from -6 to 6
- reflectors: float32 [64, 512, 256], P('row', 'vec'), may hold values from -0.25 to 0.25
- inner_factors: float32 [64, 256, 256], P('row', 'vec'), may hold values from -0.375 to 0.375
- offsets: int32 [2, 32], P(None, 'row'), may hold values from 0 to 15872, as said below
- owners: int32 [2, 32], P(None, 'row'), may hold values from 0 to 3, as said below
Outputs:
- result: float32 [16384, 6144], P('row', 'vec')
Inputs may be any that keep to these rules, and one draw needn't show every extreme that they name: `offsets`: within each sweep the columns j * 2 to (j + 1) * 2 - 1 belong to panel j, the rows j * 1024 to (j + 1) * 1024 - 1; a panel's start rows increase and are multiples of 256. A first-sweep block lies within its panel. A second-sweep block starts 256 rows or more after its panel's first row; in every panel but the last, the last second-sweep block starts at the panel's end minus 256, so it runs 256 rows into the next panel; the last panel's second-sweep blocks lie within it. `owners`: for each panel, its 4 entries (both sweeps) are a permutation of 0 to 3.
All inputs are finite; a program needn't handle non-finite values.
Results may differ from a plain program's by a relative error of at most 0.0001.
Values sent between devices are 32-bit elements; how exact they have to be, the bound alone decides.
No kernel may reach another device: no remote copies, remote signals or barrier semaphores. Data moves between devices by JAX's collectives and lax.ppermute only.
A program may use at most 64 MiB of HBM per device.

v0:
```python
import jax
import jax.numpy as jnp
from jax import lax
from jax.sharding import PartitionSpec as P


def from_behind(block, axis, distance):
    devices = range(lax.axis_size(axis))
    route = [(i - distance, i) for i in devices if i - distance in devices]
    return lax.ppermute(block, axis, route)


def contract_rows(left, right):
    return lax.dot_general(
        left,
        right,
        (((0,), (0,)), ((), ())),
        precision=lax.Precision.HIGHEST,
        preferred_element_type=jnp.float32,
    )


def multiply(left, right):
    return jnp.dot(left, right, precision=lax.Precision.HIGHEST, preferred_element_type=jnp.float32)


def shards(vectors, reflectors, inner_factors, offsets, owners):
    rows_dev = vectors.shape[0]
    reflect_count = reflectors.shape[2]
    block_rows = 2 * reflect_count
    per_sweep = offsets.shape[1]
    first_row = lax.axis_index("row") * rows_dev

    def fetch_block(owner_code):
        stored_basis = lax.dynamic_index_in_dim(reflectors, owner_code, 0, keepdims=False)
        stored_inner = lax.dynamic_index_in_dim(inner_factors, owner_code, 0, keepdims=False)
        return (
            lax.all_gather(stored_basis, "vec", axis=0, tiled=True),
            lax.all_gather(stored_inner, "vec", axis=0, tiled=True),
        )

    def run_sweep(current, sweep_index):

        def apply_block(block_index, current_rows):
            start_row = offsets[sweep_index, block_index] - first_row
            basis_block, inner_block = fetch_block(owners[sweep_index, block_index])
            window = lax.dynamic_slice_in_dim(current_rows, start_row, block_rows, 0)
            projection = contract_rows(basis_block, window)
            coupled = multiply(inner_block, projection)
            window = window - multiply(basis_block, coupled)
            return lax.dynamic_update_slice_in_dim(current_rows, window, start_row, 0)

        return lax.fori_loop(0, per_sweep, apply_block, current)

    after_first = run_sweep(vectors, 0)
    below_rows = from_behind(after_first[:reflect_count], "row", -1)
    extended = jnp.concatenate([after_first, below_rows], 0)
    extended = run_sweep(extended, 1)
    handed = from_behind(extended[rows_dev:], "row", 1)
    head_rows = jnp.where(lax.axis_index("row") > 0, handed, extended[:reflect_count])
    return jnp.concatenate([head_rows, extended[reflect_count:rows_dev]], 0)


def solution(mesh):
    return jax.shard_map(
        shards,
        mesh=mesh,
        in_specs=(
            P("row", "vec"),
            P("row", "vec", None),
            P("row", "vec", None),
            P(None, "row"),
            P(None, "row"),
        ),
        out_specs=P("row", "vec"),
        check_vma=False,
    )
```

profile of v0, /device:TPU:10, one launch (start us, length us, event | category | flops | bytes accessed | tf_op | source)
XLA Modules:
  0.0 253.6 jit_solution(5335601532820274075)
XLA Ops:
  0.0 1.4 copy-done
  1.4 109.5 %while.26 = (s32[]{:T(128)}, f32[1024,384]{1,0:T(8,128)S(1)}, s32[2,2]{1,0:T(2,128)S(1)}, s32[]{:T(128)}, s32[2,2]{1,0:T(2,128)S(1)}, /*index=5*/f32[4,32,256]{2...) while((s32[]{:T(128)}, f32[1024,384]{1,0:T(8,128)S(1)}, ...), condition=%wide.region_1.2_spmd, body=%wide.region_0.1_spmd.sunk | while | flops 1510146048 | bytes 7749873 | solution.py:53
  1.4 0.7 constant_dynamic-slice_fusion.16
  2.8 0.7 constant_dynamic-slice_fusion.17
  5.5 0.7 constant_dynamic-slice_fusion.19
  6.2 0.8 constant_dynamic-slice_fusion.18
  7.0 20.2 %all-gather.9 = f32[1,256,256]{2,1,0:T(8,128)S(1)} all-gather(f32[1,16,256]{2,1,0:T(8,128)S(1)} %constant_dynamic-slice_fusion.19), channel_id=3, replica_groups=mesh['row'=16,'vec'=16] {'vec'}, dimensions={1}, use_global_device_ids=true | all-gather | bytes 278528 | tf_op jit(solution)/shard_map/while/body/eval_jaxpr/all_gather | solution.py:39
  27.2 24.8 %all-gather.8 = f32[1,512,256]{2,1,0:T(8,128)S(1)} all-gather(f32[1,32,256]{2,1,0:T(8,128)S(1)} %constant_dynamic-slice_fusion.18), channel_id=2, replica_groups=mesh['row'=16,'vec'=16] {'vec'}, dimensions={1}, use_global_device_ids=true | all-gather | bytes 557056 | tf_op jit(solution)/shard_map/while/body/eval_jaxpr/all_gather | solution.py:38
  52.0 1.1 fusion.40
  53.7 1.0 convolution_subtract_fusion.4
  54.7 3.0 %dynamic_update_slice.16 = f32[1024,384]{1,0:T(8,128)S(1)} dynamic-update-slice(f32[1024,384]{1,0:T(8,128)S(1)} %get-tuple-element.381, f32[512,384]{1,0:T(8,128)S(1)} %convolution_subtract_fusion.4, s32[]{:T(128)S(6)} %select_n.62, s32[]{:T(128)} %constant.85.clone.1..sunk) | dynamic-update-slice | bytes 1572868 | tf_op jit(solution)/shard_map/while/body/eval_jaxpr/dynamic_update_slice | solution.py:51
  57.7 0.7 constant_dynamic-slice_fusion.16
  59.1 0.7 constant_dynamic-slice_fusion.17
  61.8 0.7 constant_dynamic-slice_fusion.19
  62.5 0.8 constant_dynamic-slice_fusion.18
  63.3 20.0 %all-gather.9 = f32[1,256,256]{2,1,0:T(8,128)S(1)} all-gather(f32[1,16,256]{2,1,0:T(8,128)S(1)} %constant_dynamic-slice_fusion.19), channel_id=3, replica_groups=mesh['row'=16,'vec'=16] {'vec'}, dimensions={1}, use_global_device_ids=true | all-gather | bytes 278528 | tf_op jit(solution)/shard_map/while/body/eval_jaxpr/all_gather | solution.py:39
  83.3 22.0 %all-gather.8 = f32[1,512,256]{2,1,0:T(8,128)S(1)} all-gather(f32[1,32,256]{2,1,0:T(8,128)S(1)} %constant_dynamic-slice_fusion.18), channel_id=2, replica_groups=mesh['row'=16,'vec'=16] {'vec'}, dimensions={1}, use_global_device_ids=true | all-gather | bytes 557056 | tf_op jit(solution)/shard_map/while/body/eval_jaxpr/all_gather | solution.py:38
  105.3 1.1 fusion.40
  106.3 0.6 fusion.41
  107.0 1.0 convolution_subtract_fusion.4
  108.0 2.9 %dynamic_update_slice.16 = f32[1024,384]{1,0:T(8,128)S(1)} dynamic-update-slice(f32[1024,384]{1,0:T(8,128)S(1)} %get-tuple-element.381, f32[512,384]{1,0:T(8,128)S(1)} %convolution_subtract_fusion.4, s32[]{:T(128)S(6)} %select_n.62, s32[]{:T(128)} %constant.85.clone.1..sunk) | dynamic-update-slice | bytes 1572868 | tf_op jit(solution)/shard_map/while/body/eval_jaxpr/dynamic_update_slice | solution.py:51
  110.9 8.5 %collective-permute-start = (f32[256,384]{1,0:T(8,128)S(1)}, f32[256,384]{1,0:T(8,128)}, u32[]{:S(2)}, u32[]{:S(2)}) collective-permute-start(f32[256,384]{1,0:T(8,128)S(1)} %slice.12), channel_id=1, source_target_pairs={{16,0},{32,16},{48,32},{64,48},{80,64},{96,80},{112,96},{128,112},... | collective-permute-start | bytes 1179656 | tf_op jit(solution)/shard_map/ppermute | solution.py:10
  119.5 8.9 %collective-permute-done = f32[256,384]{1,0:T(8,128)} collective-permute-done((f32[256,384]{1,0:T(8,128)S(1)}, f32[256,384]{1,0:T(8,128)}, u32[]{:S(2)}, u32[]{:S(2)}) %collective-permute-start) | collective-permute-done | bytes 393248 | tf_op jit(solution)/shard_map/ppermute | solution.py:10
  128.4 1.1 pad_maximum_fusion
  129.5 106.5 %while.27 = (s32[]{:T(128)}, f32[1280,384]{1,0:T(8,128)S(1)}, s32[2,2]{1,0:T(2,128)S(1)}, s32[]{:T(128)}, s32[2,2]{1,0:T(2,128)S(1)}, /*index=5*/f32[4,32,256]{2...) while((s32[]{:T(128)}, f32[1280,384]{1,0:T(8,128)S(1)}, ...), condition=%wide.region_3.4_spmd, body=%wide.region_2.3_spmd.sunk | while | flops 1510146048 | bytes 7749873 | solution.py:53
  129.5 0.7 constant_dynamic-slice_fusion.20
  130.9 0.7 constant_dynamic-slice_fusion.21
  133.6 0.7 constant_dynamic-slice_fusion.23
  134.3 0.8 constant_dynamic-slice_fusion.22
  135.1 20.0 %all-gather.11 = f32[1,256,256]{2,1,0:T(8,128)S(1)} all-gather(f32[1,16,256]{2,1,0:T(8,128)S(1)} %constant_dynamic-slice_fusion.23), channel_id=5, replica_groups=mesh['row'=16,'vec'=16] {'vec'}, dimensions={1}, use_global_device_ids=true | all-gather | bytes 278528 | tf_op jit(solution)/shard_map/while/body/eval_jaxpr/all_gather | solution.py:39
  155.1 22.0 %all-gather.10 = f32[1,512,256]{2,1,0:T(8,128)S(1)} all-gather(f32[1,32,256]{2,1,0:T(8,128)S(1)} %constant_dynamic-slice_fusion.22), channel_id=4, replica_groups=mesh['row'=16,'vec'=16] {'vec'}, dimensions={1}, use_global_device_ids=true | all-gather | bytes 557056 | tf_op jit(solution)/shard_map/while/body/eval_jaxpr/all_gather | solution.py:38
  177.1 1.1 fusion.48
  178.1 0.6 fusion.49
  178.8 1.0 convolution_subtract_fusion.5
  179.8 3.0 %dynamic_update_slice.17 = f32[1280,384]{1,0:T(8,128)S(1)} dynamic-update-slice(f32[1280,384]{1,0:T(8,128)S(1)} %get-tuple-element.414, f32[512,384]{1,0:T(8,128)S(1)} %convolution_subtract_fusion.5, s32[]{:T(128)S(6)} %select_n.64, s32[]{:T(128)} %constant.85.clone.1..sunk.1) | dynamic-update-slice | bytes 1572868 | tf_op jit(solution)/shard_map/while/body/eval_jaxpr/dynamic_update_slice | solution.py:51
  182.8 0.7 constant_dynamic-slice_fusion.20
  184.2 0.7 constant_dynamic-slice_fusion.21
  186.9 0.7 constant_dynamic-slice_fusion.23
  187.6 0.8 constant_dynamic-slice_fusion.22
  188.4 20.0 %all-gather.11 = f32[1,256,256]{2,1,0:T(8,128)S(1)} all-gather(f32[1,16,256]{2,1,0:T(8,128)S(1)} %constant_dynamic-slice_fusion.23), channel_id=5, replica_groups=mesh['row'=16,'vec'=16] {'vec'}, dimensions={1}, use_global_device_ids=true | all-gather | bytes 278528 | tf_op jit(solution)/shard_map/while/body/eval_jaxpr/all_gather | solution.py:39
  208.3 22.0 %all-gather.10 = f32[1,512,256]{2,1,0:T(8,128)S(1)} all-gather(f32[1,32,256]{2,1,0:T(8,128)S(1)} %constant_dynamic-slice_fusion.22), channel_id=4, replica_groups=mesh['row'=16,'vec'=16] {'vec'}, dimensions={1}, use_global_device_ids=true | all-gather | bytes 557056 | tf_op jit(solution)/shard_map/while/body/eval_jaxpr/all_gather | solution.py:38
  230.4 1.1 fusion.48
  231.4 0.6 fusion.49
  232.0 1.0 convolution_subtract_fusion.5
  233.0 2.9 %dynamic_update_slice.17 = f32[1280,384]{1,0:T(8,128)S(1)} dynamic-update-slice(f32[1280,384]{1,0:T(8,128)S(1)} %get-tuple-element.414, f32[512,384]{1,0:T(8,128)S(1)} %convolution_subtract_fusion.5, s32[]{:T(128)S(6)} %select_n.64, s32[]{:T(128)} %constant.85.clone.1..sunk.1) | dynamic-update-slice | bytes 1572868 | tf_op jit(solution)/shard_map/while/body/eval_jaxpr/dynamic_update_slice | solution.py:51
  236.0 1.9 collective-permute-start.1
  238.1 14.2 %collective-permute-done.1 = f32[256,384]{1,0:T(8,128)S(1)} collective-permute-done((f32[256,384]{1,0:T(8,128)S(1)}, f32[256,384]{1,0:T(8,128)S(1)}, u32[]{:S(2)}, u32[]{:S(2)}) %collective-permute-start.1) | collective-permute-done | bytes 393248 | tf_op jit(solution)/shard_map/ppermute | solution.py:10
  252.3 1.2 pad_maximum_fusion.1
  (10 shorter events, 0.8 us)
Async XLA Ops:
  0.0 1.4 copy-start
  0.0 1.4 copy-start.1
  0.0 1.4 copy-start.2
  110.9 17.4 %collective-permute-start = (f32[256,384]{1,0:T(8,128)S(1)}, f32[256,384]{1,0:T(8,128)}, u32[]{:S(2)}, u32[]{:S(2)}) collective-permute-start(f32[256,384]{1,0:T(8,128)S(1)} %slice.12), channel_id=1, source_target_pairs={{16,0},{32,16},{48,32},{64,48},{80,64},{96,80},{112,96},{128,112},... | collective-permute-start | bytes 1179656 | tf_op jit(solution)/shard_map/ppermute | solution.py:10
  236.0 16.2 %collective-permute-start.1 = (f32[256,384]{1,0:T(8,128)S(1)}, f32[256,384]{1,0:T(8,128)S(1)}, u32[]{:S(2)}, u32[]{:S(2)}) collective-permute-start(f32[256,384]{1,0:T(8,128)S(1)} %slice.13), channel_id=1, source_target_pairs={{0,16},{16,32},{32,48},{48,64},{64,80},{80,96},{96,112},{112,128},... | collective-permute-start | bytes 1179656 | tf_op jit(solution)/shard_map/ppermute | solution.py:10
where the time goes:
time: 254 us
  blocking collectives  171 us (67%)
  local copies, waits for them, and re-layouts  24.7 us (10%)
  waiting for transfers between devices  23.1 us (9%)
  loops' own time  11.3 us (4%)
  matrix products  10.6 us (4%)
  starting transfers between devices  10.5 us (4%)
    all_gather x4, blocking collectives, fetch_block(): lax.all_gather(stored_basis, 'vec', axis=0, tiled=True)  90.9 us
    all_gather x4, blocking collectives, fetch_block(): lax.all_gather(stored_inner, 'vec', axis=0, tiled=True)  80 us
    ppermute x2, waiting for transfers between devices, from_behind(): return lax.ppermute(block, axis, route)  23.1 us
    dynamic_update_slice x4, local copies, waits for them, and re-layouts, apply_block(): return lax.dynamic_update_slice_in_dim(current_rows, window, start_row, 0)  11.9 us
    another operation x2, loops' own time, run_sweep(): return lax.fori_loop(0, per_sweep, apply_block, current)  11.3 us
    ppermute x2, starting transfers between devices, from_behind(): return lax.ppermute(block, axis, route)  10.5 us
    dot_general x8, matrix products, multiply(): jnp.dot(left, right, precision=lax.Precision.HIGHEST, preferred_element_t...  6.36 us
  transfers between devices with their start and end apart: 2, of which 2 were waited for; matrix products, arithmetic and copies ran while one was open for 0% of the time, Pallas kernels for 0%

commit v1 on v0

v1 whole, which is shorter than its diff:
```python
import functools

import jax
import jax.numpy as jnp
from jax import lax
from jax.experimental import pallas as pl
from jax.experimental.pallas import tpu as pltpu
from jax.sharding import PartitionSpec as P

ROW, VEC = "row", "vec"
Y, X, C = 2, 4, 2
FIRST = 1
BASIS, INNER = 32, 16
PIECE = BASIS + INNER
STEP = 256
ROWS = 1024
VMEM = pl.BlockSpec(memory_space=pltpu.VMEM)
SMEM = pl.BlockSpec(memory_space=pltpu.SMEM)
ANY = pl.BlockSpec(memory_space=pl.ANY)


def index_of(y, x, c):
    return (y * X + x) * C + c


def routes(target):
    pairs = []
    for y in range(Y):
        for x in range(X):
            for c in range(C):
                ty, tx, tc = target(y, x, c)
                pairs.append((index_of(y, x, c), index_of(ty % Y, tx % X, tc)))
    return pairs


def side(c):
    return 1 - 2 * c


SWAP = routes(lambda y, x, c: (y, x, 1 - c))
NEAR = routes(lambda y, x, c: (y, x + side(c), c))
CROSS = routes(lambda y, x, c: (y + 1, x + side(c), c))
FAR = routes(lambda y, x, c: (y, x + 2, c) if c == 0 else (y + 1, x, c))
LAST = routes(lambda y, x, c: (y + 1, x + 2, c))


def send(block, route):
    return lax.ppermute(block, VEC, route)


def collect(own, other):
    chip = jnp.concatenate([own, other], 0)
    received = [send(chip, NEAR), send(chip, CROSS), send(chip, FAR), send(own, LAST)]
    swapped = [send(block, SWAP) for block in received]
    return [own, other, *received, *swapped]


def sources(vec):
    c = lax.rem(vec, C)
    x = lax.rem(vec // C, X)
    y = vec // (C * X)
    d = side(c)

    def at(dy, dx, dc):
        return index_of(lax.rem(y + dy, Y), lax.rem(x + dx + X, X), lax.rem(c + dc, C))

    far_y, far_x = c, 2 - 2 * c
    return [
        [at(0, 0, 0)],
        [at(0, 0, 1)],
        [at(0, -d, 0), at(0, -d, 1)],
        [at(1, -d, 0), at(1, -d, 1)],
        [at(far_y, far_x, 0), at(far_y, far_x, 1)],
        [at(1, 2, 0)],
        [at(0, d, 1), at(0, d, 0)],
        [at(1, d, 1), at(1, d, 0)],
        [at(1 - far_y, 2 - far_x, 1), at(1 - far_y, 2 - far_x, 0)],
        [at(1, 2, 1)],
    ]


def split(value):
    high = value.astype(jnp.bfloat16)
    low = (value - high.astype(jnp.float32)).astype(jnp.bfloat16)
    return high, low


def product(left, right, dims):
    dot = functools.partial(
        lax.dot_general, dimension_numbers=(dims, ((), ())), preferred_element_type=jnp.float32
    )
    return dot(left[0], right[0]) + (dot(left[0], right[1]) + dot(left[1], right[0]))


def order_kernel(owners, reflectors, inner, out):
    for sweep in range(2):
        for block in range(2):
            code = owners[sweep, block]
            at = (sweep * 2 + block) * PIECE
            out[at : at + BASIS] = reflectors[code]
            out[at + BASIS : at + PIECE] = inner[code]


def apply_blocks(first_row, vec, starts, pieces, work, basis, inner, b0=0):
    places = sources(vec)
    n_blocks = len(starts)
    for b in range(n_blocks):
        for ref, owners in zip(pieces, places, strict=True):
            rows = ref.shape[0] // len(owners)
            for i, device in enumerate(owners):
                at = i * rows + b * PIECE
                high, low = split(ref[at : at + PIECE, :])
                to = pl.ds(pl.multiple_of(device * BASIS, BASIS), BASIS)
                basis[b, 0, to, :] = high[:BASIS]
                basis[b, 1, to, :] = low[:BASIS]
                to = pl.ds(pl.multiple_of(device * INNER, INNER), INNER)
                inner[b, 0, to, :] = high[BASIS:]
                inner[b, 1, to, :] = low[BASIS:]
    for b, start in enumerate(starts):
        window = pl.ds(pl.multiple_of(start - first_row, STEP), 2 * STEP)
        v = (basis[b, 0], basis[b, 1])
        s = (inner[b, 0], inner[b, 1])
        old = work[window, :]
        projection = product(v, split(old), ((0,), (0,)))
        coupled = product(s, split(projection), ((1,), (0,)))
        work[window, :] = old - product(v, split(coupled), ((1,), (0,)))


def first_kernel(n, position, offsets, vectors, *refs):
    pieces, (out, head, basis, inner) = refs[:-4], refs[-4:]
    out[...] = vectors[...]
    starts = [offsets[b // 2, b % 2] for b in range(n)]
    apply_blocks(position[0] * ROWS, position[1], starts, pieces, out, basis, inner)
    head[...] = out[:STEP, :]


def second_kernel(n, position, offsets, vectors, below, *refs):
    pieces, (out, handed, work, basis, inner) = refs[:-5], refs[-5:]
    work[:ROWS, :] = vectors[...]
    work[ROWS:, :] = below[...]
    starts = [offsets[b // 2, b % 2] for b in range(4 - n, 4)]
    apply_blocks(position[0] * ROWS, position[1], starts, pieces, work, basis, inner)
    handed[...] = work[ROWS:, :]
    out[...] = work[:ROWS, :]


def finish_kernel(position, handed, body, out, sem):
    del body

    @pl.when(position[0] > 0)
    def _():
        copy = pltpu.make_async_copy(handed, out.at[:STEP, :], sem)
        copy.start()
        copy.wait()


def neighbour(block, step):
    size = lax.axis_size(ROW)
    return lax.ppermute(block, ROW, [(i, i + step) for i in range(size) if 0 <= i + step < size])


def shards(vectors, reflectors, inner_factors, offsets, owners):
    columns = vectors.shape[1]
    f32 = jnp.float32
    position = jnp.stack([lax.axis_index(ROW), lax.axis_index(VEC)]).astype(jnp.int32)

    def scratch(n):
        return [
            pltpu.VMEM((n, 2, 2 * STEP, STEP), jnp.bfloat16),
            pltpu.VMEM((n, 2, STEP, STEP), jnp.bfloat16),
        ]

    def cost(n):
        return pl.CostEstimate(flops=n * 3 * 250_000_000, bytes_accessed=4_000_000, transcendentals=0)

    own = pl.pallas_call(
        order_kernel,
        out_shape=jax.ShapeDtypeStruct((4 * PIECE, STEP), f32),
        in_specs=[SMEM, VMEM, VMEM],
        out_specs=VMEM,
    )(owners, reflectors, inner_factors)
    cut = FIRST * PIECE
    other = send(own, SWAP)
    early = collect(own[:cut], other[:cut])
    late = collect(own[cut:], other[cut:])

    n = FIRST
    current, head = pl.pallas_call(
        functools.partial(first_kernel, n),
        out_shape=(jax.ShapeDtypeStruct(vectors.shape, f32), jax.ShapeDtypeStruct((STEP, columns), f32)),
        in_specs=[SMEM, SMEM, VMEM] + [VMEM] * len(early),
        out_specs=(VMEM, VMEM),
        scratch_shapes=scratch(n),
        cost_estimate=cost(n),
    )(position, offsets, vectors, *early)
    below = neighbour(head, -1)

    n = 4 - FIRST
    body, handed = pl.pallas_call(
        functools.partial(second_kernel, n),
        out_shape=(jax.ShapeDtypeStruct(vectors.shape, f32), jax.ShapeDtypeStruct((STEP, columns), f32)),
        in_specs=[SMEM, SMEM, VMEM, VMEM] + [VMEM] * len(late),
        out_specs=(VMEM, VMEM),
        scratch_shapes=[pltpu.VMEM((ROWS + STEP, columns), f32)] + scratch(n),
        cost_estimate=cost(n),
    )(position, offsets, current, below, *late)
    arrived = neighbour(handed, 1)

    return pl.pallas_call(
        finish_kernel,
        out_shape=jax.ShapeDtypeStruct(vectors.shape, f32),
        in_specs=[SMEM, ANY, ANY],
        out_specs=ANY,
        scratch_shapes=[pltpu.SemaphoreType.DMA],
        input_output_aliases={2: 0},
    )(position, arrived, body)


def solution(mesh):
    return jax.shard_map(
        shards,
        mesh=mesh,
        in_specs=(
            P(ROW, VEC),
            P(ROW, VEC, None),
            P(ROW, VEC, None),
            P(None, ROW),
            P(None, ROW),
        ),
        out_specs=P(ROW, VEC),
        check_vma=False,
    )
```

time: 254 us -> 91.5 us (0.36)
  blocking collectives: 171 us -> 0 us
  Pallas kernels: 0 us -> 28.1 us
  local copies, waits for them, and re-layouts: 24.7 us -> 4.43 us
  starting transfers between devices: 10.5 us -> 29.5 us
  loops' own time: 11.3 us -> 0 us
  matrix products: 10.6 us -> 0 us
  waiting for transfers between devices: 23.1 us -> 27.2 us
    all_gather x8 -> x0, blocking collectives: 171 us -> none  [the longest x4 90.9 us: fetch_block(): lax.all_gather(stored_basis, 'vec', axis=0, tiled=True)]
    pallas_call x0 -> x4, Pallas kernels: none -> 28.1 us  [the longest x1 13.7 us: shards(): pl.pallas_call(finish_kernel, out_shape=jax.ShapeDtypeStruct(vectors.shap...]
    ppermute x2 -> x19, starting transfers between devices: 10.5 us -> 29.5 us  [the longest x17 19.1 us: send(): return lax.ppermute(block, VEC, route)]
    dynamic_update_slice x4 -> x0, local copies, waits for them, and re-layouts: 11.9 us -> none  [apply_block(): return lax.dynamic_update_slice_in_dim(current_rows, window, start_row, 0)]
    another operation x2 -> x0, loops' own time: 11.3 us -> none  [run_sweep(): return lax.fori_loop(0, per_sweep, apply_block, current)]
    dynamic_slice x16 -> x0, local copies, waits for them, and re-layouts: 11.3 us -> none  [the longest x4 3.04 us: fetch_block(): lax.dynamic_index_in_dim(reflectors, owner_code, 0, keepdims=False)]
    dot_general x12 -> x0, matrix products: 10.6 us -> none  [the longest x8 6.36 us: multiply(): jnp.dot(left, right, precision=lax.Precision.HIGHEST, preferred_element_t...]
    ppermute x2 -> x19, waiting for transfers between devices: 23.1 us -> 27.2 us  [the longest x2 14.5 us: neighbour(): lax.ppermute(block, ROW, [(i, i + step) for i in range(size) if 0 <= i +...]
  transfers between devices with their start and end apart: 2 -> 19, of which waited for: 2 -> 9; matrix products, arithmetic and copies ran while one was open for 0% -> 3% of each run, Pallas kernels for 0% -> 5%
where the time goes in v1:
time: 91.5 us; the launch traced here: 90.3 us
  starting transfers between devices  29.5 us (32%)
  Pallas kernels  28.1 us (31%)
  waiting for transfers between devices  27.2 us (30%)
  local copies, waits for them, and re-layouts  4.43 us (5%)
    ppermute x17, starting transfers between devices, send(): return lax.ppermute(block, VEC, route)  19.1 us
    ppermute x2, waiting for transfers between devices, neighbour(): lax.ppermute(block, ROW, [(i, i + step) for i in range(size) if 0 <= i +...  14.5 us
    pallas_call x1, Pallas kernels, shards(): pl.pallas_call(finish_kernel, out_shape=jax.ShapeDtypeStruct(vectors.shap...  13.7 us
    ppermute x17, waiting for transfers between devices, send(): return lax.ppermute(block, VEC, route)  12.7 us
    ppermute x2, starting transfers between devices, neighbour(): lax.ppermute(block, ROW, [(i, i + step) for i in range(size) if 0 <= i +...  10.4 us
    pallas_call x1, Pallas kernels, shards(): pl.pallas_call(functools.partial(second_kernel, n), out_shape=(jax.ShapeD...  8.25 us
    pallas_call x1, Pallas kernels, shards(): pl.pallas_call(functools.partial(first_kernel, n), out_shape=(jax.ShapeDt...  4.58 us
    unnamed x44, local copies, waits for them, and re-layouts  2.69 us
  transfers between devices with their start and end apart: 19, of which 9 were waited for; matrix products, arithmetic and copies ran while one was open for 3% of the time, Pallas kernels for 5%

profile of v1, /device:TPU:10, one launch (start us, length us, event | category | flops | bytes accessed | tf_op | source)
XLA Modules:
  0.0 90.3 jit_solution(11366788670328898087)
XLA Ops:
  0.0 1.6 %shard_map.55 = f32[192,256]{1,0:T(8,128)} custom-call(s32[2,2]{1,0:T(2,128)} %owners.1, f32[4,32,256]{2,1,0:T(8,128)} %reflectors.1, f32[4,16,256]{2,1,0:T(8,128)} %inner.1), custom_call_target="tpu_custom_call" | custom-call | tf_op jit(solution)/shard_map/pallas_call | solution.py:176
  1.6 0.0 collective-permute-start
  1.6 0.8 slice.16.refs_0_
  2.4 0.8 collective-permute-done
  3.3 2.2 %collective-permute-start.3 = (f32[96,256]{1,0:T(8,128)S(1)}, f32[96,256]{1,0:T(8,128)S(1)}, u32[]{:S(2)}, u32[]{:S(2)}) collective-permute-start(f32[96,256]{1,0:T(8,128)S(1)} %pad_maximum_fusion.1), channel_id=1, source_target_pairs={{0,4},{1,9},{2,6},{3,11},{4,0},{5,13},{6,2},{7,15},{8,12},{9,1},{1... | collective-permute-start | bytes 294920 | tf_op jit(solution)/shard_map/ppermute | solution.py:48
  5.5 3.1 %collective-permute-start.4 = (f32[48,256]{1,0:T(8,128)S(1)}, f32[48,256]{1,0:T(8,128)S(1)}, u32[]{:S(2)}, u32[]{:S(2)}) collective-permute-start(f32[48,256]{1,0:T(8,128)S(1)} %slice.16.refs_0_), channel_id=1, source_target_pairs={{0,12},{1,13},{2,14},{3,15},{4,8},{5,9},{6,10},{7,11},{8,4},{9,5},... | collective-permute-start | bytes 147464 | tf_op jit(solution)/shard_map/ppermute | solution.py:48
  8.6 0.9 %slice.18.refs_0_ = f32[144,256]{1,0:T(8,128)S(1)} slice(f32[192,256]{1,0:T(8,128)} %shard_map.55), slice={[48:192], [0:256]} | slice | bytes 294912 | tf_op jit(solution)/shard_map/slice | solution.py:185
  9.6 3.9 %collective-permute-done.4.refs_5_ = f32[48,256]{1,0:T(8,128)S(1)} collective-permute-done((f32[48,256]{1,0:T(8,128)S(1)}, f32[48,256]{1,0:T(8,128)S(1)}, u32[]{:S(2)}, u32[]{:S(2)}) %collective-permute-start.4) | collective-permute-done | bytes 49184 | tf_op jit(solution)/shard_map/ppermute | solution.py:48
  13.5 0.0 collective-permute-start.8
  13.5 1.7 %collective-permute-start.2 = (f32[96,256]{1,0:T(8,128)S(1)}, f32[96,256]{1,0:T(8,128)S(1)}, u32[]{:S(2)}, u32[]{:S(2)}) collective-permute-start(f32[96,256]{1,0:T(8,128)S(1)} %pad_maximum_fusion.1), channel_id=1, source_target_pairs={{0,10},{1,15},{2,12},{3,9},{4,14},{5,11},{6,8},{7,13},{8,2},{9,7},... | collective-permute-start | bytes 294920 | tf_op jit(solution)/shard_map/ppermute | solution.py:48
  15.2 2.0 %collective-permute-start.1 = (f32[96,256]{1,0:T(8,128)S(1)}, f32[96,256]{1,0:T(8,128)S(1)}, u32[]{:S(2)}, u32[]{:S(2)}) collective-permute-start(f32[96,256]{1,0:T(8,128)S(1)} %pad_maximum_fusion.1), channel_id=1, source_target_pairs={{0,2},{1,7},{2,4},{3,1},{4,6},{5,3},{6,0},{7,5},{8,10},{9,15},{10,... | collective-permute-start | bytes 294920 | tf_op jit(solution)/shard_map/ppermute | solution.py:48
  17.2 0.0 collective-permute-done.3.refs_4_
  17.2 0.6 collective-permute-start.7
  17.9 1.7 %collective-permute-start.12 = (f32[288,256]{1,0:T(8,128)S(1)}, f32[288,256]{1,0:T(8,128)S(1)}, u32[]{:S(2)}, u32[]{:S(2)}) collective-permute-start(f32[288,256]{1,0:T(8,128)S(1)} %pad_maximum_fusion), channel_id=1, source_target_pairs={{0,4},{1,9},{2,6},{3,11},{4,0},{5,13},{6,2},{7,15},{8,12},{9,1},{1... | collective-permute-start | bytes 884744 | tf_op jit(solution)/shard_map/ppermute | solution.py:48
  19.6 0.0 collective-permute-done.8.refs_9_
  19.6 1.1 %collective-permute-start.11 = (f32[288,256]{1,0:T(8,128)S(1)}, f32[288,256]{1,0:T(8,128)S(1)}, u32[]{:S(2)}, u32[]{:S(2)}) collective-permute-start(f32[288,256]{1,0:T(8,128)S(1)} %pad_maximum_fusion), channel_id=1, source_target_pairs={{0,10},{1,15},{2,12},{3,9},{4,14},{5,11},{6,8},{7,13},{8,2},{9,7},... | collective-permute-start | bytes 884744 | tf_op jit(solution)/shard_map/ppermute | solution.py:48
  20.7 0.4 collective-permute-done.2.refs_3_
  21.1 2.0 %collective-permute-start.10 = (f32[288,256]{1,0:T(8,128)S(1)}, f32[288,256]{1,0:T(8,128)S(1)}, u32[]{:S(2)}, u32[]{:S(2)}) collective-permute-start(f32[288,256]{1,0:T(8,128)S(1)} %pad_maximum_fusion), channel_id=1, source_target_pairs={{0,2},{1,7},{2,4},{3,1},{4,6},{5,3},{6,0},{7,5},{8,10},{9,15},{10,... | collective-permute-start | bytes 884744 | tf_op jit(solution)/shard_map/ppermute | solution.py:48
  23.1 0.3 collective-permute-start.6
  23.4 0.0 collective-permute-done.7.refs_8_
  23.4 0.2 collective-permute-start.5
  23.6 0.6 pad_add_fusion.position
  24.2 0.1 collective-permute-done.6.refs_7_
  24.4 0.3 collective-permute-done.5.refs_6_
  24.8 0.3 copy-done.18
  25.0 0.6 copy-done.19
  25.7 4.6 %shard_map.56 = (f32[1024,384]{1,0:T(8,128)}, f32[256,384]{1,0:T(8,128)}) custom-call(s32[2]{0:T(128)} %pad_add_fusion.position, s32[2,2]{1,0:T(2,128)} %offsets.3, f32[1024,384]{1,0:T(8,128)} %vectors.1, f32[48,256]{1,0:T(8,128)} %copy-done.3, f32[48,256]{1,0:T(8,128)} %copy-done.4, f32[96,256]{1,0:T(8,128)} %copy-done.16, f32[96,256]{1,0:T(8,128)} %copy-done.15, ...), custom_call_target="tpu_custom_call" | custom-call | flops 750000000 | bytes 4000000 | tf_op jit(solution)/shard_map/pallas_call | solution.py:188
  30.3 8.5 %collective-permute-start.9 = (f32[256,384]{1,0:T(8,128)}, f32[256,384]{1,0:T(8,128)S(1)}, u32[]{:S(2)}, u32[]{:S(2)}) collective-permute-start(f32[256,384]{1,0:T(8,128)} %get-tuple-element.10), channel_id=1, source_target_pairs={{16,0},{32,16},{48,32},{64,48},{80,64},{96,80},{112,96},{128,112},... | collective-permute-start | bytes 1179656 | tf_op jit(solution)/shard_map/ppermute | solution.py:159
  38.8 3.5 %collective-permute-start.13 = (f32[144,256]{1,0:T(8,128)S(1)}, f32[144,256]{1,0:T(8,128)S(1)}, u32[]{:S(2)}, u32[]{:S(2)}) collective-permute-start(f32[144,256]{1,0:T(8,128)S(1)} %slice.18.refs_0_), channel_id=1, source_target_pairs={{0,12},{1,13},{2,14},{3,15},{4,8},{5,9},{6,10},{7,11},{8,4},{9,5},... | collective-permute-start | bytes 442376 | tf_op jit(solution)/shard_map/ppermute | solution.py:48
  42.3 0.0 collective-permute-done.11.refs_3_
  42.3 0.5 collective-permute-start.15
  42.8 0.0 collective-permute-done.10.refs_2_
  42.8 0.1 collective-permute-start.14
  42.9 5.7 %collective-permute-done.13.refs_5_ = f32[144,256]{1,0:T(8,128)S(1)} collective-permute-done((f32[144,256]{1,0:T(8,128)S(1)}, f32[144,256]{1,0:T(8,128)S(1)}, u32[]{:S(2)}, u32[]{:S(2)}) %collective-permute-start.13) | collective-permute-done | bytes 147488 | tf_op jit(solution)/shard_map/ppermute | solution.py:48
  48.6 0.0 collective-permute-start.17
  48.6 1.4 %collective-permute-done.17.refs_9_ = f32[144,256]{1,0:T(8,128)S(1)} collective-permute-done((f32[144,256]{1,0:T(8,128)S(1)}, f32[144,256]{1,0:T(8,128)S(1)}, u32[]{:S(2)}, u32[]{:S(2)}) %collective-permute-start.17) | collective-permute-done | bytes 147488 | tf_op jit(solution)/shard_map/ppermute | solution.py:48
  50.0 1.1 %collective-permute-done.9.below = f32[256,384]{1,0:T(8,128)S(1)} collective-permute-done((f32[256,384]{1,0:T(8,128)}, f32[256,384]{1,0:T(8,128)S(1)}, u32[]{:S(2)}, u32[]{:S(2)}) %collective-permute-start.9) | collective-permute-done | bytes 393248 | tf_op jit(solution)/shard_map/ppermute | solution.py:159
  51.0 0.0 collective-permute-done.16.refs_8_
  51.0 0.0 collective-permute-done.15.refs_7_
  51.1 0.7 copy-done.5
  51.8 0.1 copy-done.9
  51.9 0.1 copy-done.10
  52.0 0.1 copy-done.11
  52.1 8.3 %shard_map.57 = (f32[1024,384]{1,0:T(8,128)}, f32[256,384]{1,0:T(8,128)}) custom-call(s32[2]{0:T(128)} %pad_add_fusion.position, s32[2,2]{1,0:T(2,128)} %offsets.3, f32[1024,384]{1,0:T(8,128)} %get-tuple-element.9.vectors, f32[256,384]{1,0:T(8,128)} %copy-done.5, f32[144,256]{1,0:T(8,128)} %copy-done, f32[144,256]{1,0:T(8,128)} %copy-done.1, ...), custom_call_target="tpu_custom_call" | custom-call | flops 2249999872 | bytes 4000000 | tf_op jit(solution)/shard_map/pallas_call | solution.py:199
  60.4 1.9 %collective-permute-start.18 = (f32[256,384]{1,0:T(8,128)}, f32[256,384]{1,0:T(8,128)S(1)}, u32[]{:S(2)}, u32[]{:S(2)}) collective-permute-start(f32[256,384]{1,0:T(8,128)} %get-tuple-element.11), channel_id=1, source_target_pairs={{0,16},{16,32},{32,48},{48,64},{64,80},{80,96},{96,112},{112,128},... | collective-permute-start | bytes 1179656 | tf_op jit(solution)/shard_map/ppermute | solution.py:159
  62.3 13.4 %collective-permute-done.18.handed = f32[256,384]{1,0:T(8,128)S(1)} collective-permute-done((f32[256,384]{1,0:T(8,128)}, f32[256,384]{1,0:T(8,128)S(1)}, u32[]{:S(2)}, u32[]{:S(2)}) %collective-permute-start.18) | collective-permute-done | bytes 393248 | tf_op jit(solution)/shard_map/ppermute | solution.py:159
  75.7 0.7 copy-done.2
  76.5 13.7 %shard_map.58 = f32[1024,384]{1,0:T(8,128)} custom-call(s32[2]{0:T(128)} %pad_add_fusion.position, f32[256,384]{1,0:T(8,128)} %copy-done.2, f32[1024,384]{1,0:T(8,128)} %get-tuple-element.12.body), custom_call_target="tpu_custom_call", output_to_operand_aliasing={{}: (2, {})} | custom-call | tf_op jit(solution)/shard_map/pallas_call | solution.py:209
  (45 shorter events, 0.1 us)
Async XLA Ops:
  1.6 1.7 %collective-permute-start = (f32[192,256]{1,0:T(8,128)}, f32[192,256]{1,0:T(8,128)S(1)}, u32[]{:S(2)}, u32[]{:S(2)}) collective-permute-start(f32[192,256]{1,0:T(8,128)} %shard_map.55), channel_id=1, source_target_pairs={{0,1},{1,0},{2,3},{3,2},{4,5},{5,4},{6,7},{7,6},{8,9},{9,8},{10,11... | collective-permute-start | bytes 589832 | tf_op jit(solution)/shard_map/ppermute | solution.py:48
  2.4 22.3 %copy-start.3 = (f32[48,256]{1,0:T(8,128)}, f32[48,256]{1,0:T(8,128)S(1)}, u32[]{:S(2)}) copy-start(f32[48,256]{1,0:T(8,128)S(1)} %slice.16.refs_0_) | copy-start | bytes 147460
  3.3 21.4 %copy-start.4 = (f32[48,256]{1,0:T(8,128)}, f32[48,256]{1,0:T(8,128)S(1)}, u32[]{:S(2)}) copy-start(f32[48,256]{1,0:T(8,128)S(1)} %slice.17.refs_1_) | copy-start | bytes 147460
  3.3 13.9 %collective-permute-start.3 = (f32[96,256]{1,0:T(8,128)S(1)}, f32[96,256]{1,0:T(8,128)S(1)}, u32[]{:S(2)}, u32[]{:S(2)}) collective-permute-start(f32[96,256]{1,0:T(8,128)S(1)} %pad_maximum_fusion.1), channel_id=1, source_target_pairs={{0,4},{1,9},{2,6},{3,11},{4,0},{5,13},{6,2},{7,15},{8,12},{9,1},{1... | collective-permute-start | bytes 294920 | tf_op jit(solution)/shard_map/ppermute | solution.py:48
  5.5 8.0 %collective-permute-start.4 = (f32[48,256]{1,0:T(8,128)S(1)}, f32[48,256]{1,0:T(8,128)S(1)}, u32[]{:S(2)}, u32[]{:S(2)}) collective-permute-start(f32[48,256]{1,0:T(8,128)S(1)} %slice.16.refs_0_), channel_id=1, source_target_pairs={{0,12},{1,13},{2,14},{3,15},{4,8},{5,9},{6,10},{7,11},{8,4},{9,5},... | collective-permute-start | bytes 147464 | tf_op jit(solution)/shard_map/ppermute | solution.py:48
  9.6 29.2 %copy-start = (f32[144,256]{1,0:T(8,128)}, f32[144,256]{1,0:T(8,128)S(1)}, u32[]{:S(2)}) copy-start(f32[144,256]{1,0:T(8,128)S(1)} %slice.18.refs_0_) | copy-start | bytes 442372
  13.5 11.2 %copy-start.20 = (f32[48,256]{1,0:T(8,128)}, f32[48,256]{1,0:T(8,128)S(1)}, u32[]{:S(2)}) copy-start(f32[48,256]{1,0:T(8,128)S(1)} %collective-permute-done.4.refs_5_) | copy-start | bytes 147460
  13.5 6.1 %collective-permute-start.8 = (f32[48,256]{1,0:T(8,128)S(1)}, f32[48,256]{1,0:T(8,128)S(1)}, u32[]{:S(2)}, u32[]{:S(2)}) collective-permute-start(f32[48,256]{1,0:T(8,128)S(1)} %collective-permute-done.4.refs_5_), channel_id=1, source_target_pairs={{0,1},{1,0},{2,3},{3,2},{4,5},{5,4},{6,7},{7,6},{8,9},{9,8},{10,11... | collective-permute-start | bytes 147464 | tf_op jit(solution)/shard_map/ppermute | solution.py:48
  13.5 7.6 %collective-permute-start.2 = (f32[96,256]{1,0:T(8,128)S(1)}, f32[96,256]{1,0:T(8,128)S(1)}, u32[]{:S(2)}, u32[]{:S(2)}) collective-permute-start(f32[96,256]{1,0:T(8,128)S(1)} %pad_maximum_fusion.1), channel_id=1, source_target_pairs={{0,10},{1,15},{2,12},{3,9},{4,14},{5,11},{6,8},{7,13},{8,2},{9,7},... | collective-permute-start | bytes 294920 | tf_op jit(solution)/shard_map/ppermute | solution.py:48
  15.2 7.8 %collective-permute-start.1 = (f32[96,256]{1,0:T(8,128)S(1)}, f32[96,256]{1,0:T(8,128)S(1)}, u32[]{:S(2)}, u32[]{:S(2)}) collective-permute-start(f32[96,256]{1,0:T(8,128)S(1)} %pad_maximum_fusion.1), channel_id=1, source_target_pairs={{0,2},{1,7},{2,4},{3,1},{4,6},{5,3},{6,0},{7,5},{8,10},{9,15},{10,... | collective-permute-start | bytes 294920 | tf_op jit(solution)/shard_map/ppermute | solution.py:48
  17.2 13.0 %copy-start.1 = (f32[144,256]{1,0:T(8,128)}, f32[144,256]{1,0:T(8,128)S(1)}, u32[]{:S(2)}) copy-start(f32[144,256]{1,0:T(8,128)S(1)} %slice.19.refs_1_) | copy-start | bytes 442372
  17.2 7.5 %copy-start.14 = (f32[96,256]{1,0:T(8,128)}, f32[96,256]{1,0:T(8,128)S(1)}, u32[]{:S(2)}) copy-start(f32[96,256]{1,0:T(8,128)S(1)} %collective-permute-done.3.refs_4_) | copy-start | bytes 294916
  17.2 6.1 %collective-permute-start.7 = (f32[96,256]{1,0:T(8,128)S(1)}, f32[96,256]{1,0:T(8,128)S(1)}, u32[]{:S(2)}, u32[]{:S(2)}) collective-permute-start(f32[96,256]{1,0:T(8,128)S(1)} %collective-permute-done.3.refs_4_), channel_id=1, source_target_pairs={{0,1},{1,0},{2,3},{3,2},{4,5},{5,4},{6,7},{7,6},{8,9},{9,8},{10,11... | collective-permute-start | bytes 294920 | tf_op jit(solution)/shard_map/ppermute | solution.py:48
  17.9 24.4 %collective-permute-start.12 = (f32[288,256]{1,0:T(8,128)S(1)}, f32[288,256]{1,0:T(8,128)S(1)}, u32[]{:S(2)}, u32[]{:S(2)}) collective-permute-start(f32[288,256]{1,0:T(8,128)S(1)} %pad_maximum_fusion), channel_id=1, source_target_pairs={{0,4},{1,9},{2,6},{3,11},{4,0},{5,13},{6,2},{7,15},{8,12},{9,1},{1... | collective-permute-start | bytes 884744 | tf_op jit(solution)/shard_map/ppermute | solution.py:48
  19.6 5.1 %copy-start.21 = (f32[48,256]{1,0:T(8,128)}, f32[48,256]{1,0:T(8,128)S(1)}, u32[]{:S(2)}) copy-start(f32[48,256]{1,0:T(8,128)S(1)} %collective-permute-done.8.refs_9_) | copy-start | bytes 147460
  19.6 22.7 %collective-permute-start.11 = (f32[288,256]{1,0:T(8,128)S(1)}, f32[288,256]{1,0:T(8,128)S(1)}, u32[]{:S(2)}, u32[]{:S(2)}) collective-permute-start(f32[288,256]{1,0:T(8,128)S(1)} %pad_maximum_fusion), channel_id=1, source_target_pairs={{0,10},{1,15},{2,12},{3,9},{4,14},{5,11},{6,8},{7,13},{8,2},{9,7},... | collective-permute-start | bytes 884744 | tf_op jit(solution)/shard_map/ppermute | solution.py:48
  21.1 3.6 %copy-start.15 = (f32[96,256]{1,0:T(8,128)}, f32[96,256]{1,0:T(8,128)S(1)}, u32[]{:S(2)}) copy-start(f32[96,256]{1,0:T(8,128)S(1)} %collective-permute-done.2.refs_3_) | copy-start | bytes 294916
  21.1 21.7 %collective-permute-start.10 = (f32[288,256]{1,0:T(8,128)S(1)}, f32[288,256]{1,0:T(8,128)S(1)}, u32[]{:S(2)}, u32[]{:S(2)}) collective-permute-start(f32[288,256]{1,0:T(8,128)S(1)} %pad_maximum_fusion), channel_id=1, source_target_pairs={{0,2},{1,7},{2,4},{3,1},{4,6},{5,3},{6,0},{7,5},{8,10},{9,15},{10,... | collective-permute-start | bytes 884744 | tf_op jit(solution)/shard_map/ppermute | solution.py:48
  23.1 1.7 %copy-start.16 = (f32[96,256]{1,0:T(8,128)}, f32[96,256]{1,0:T(8,128)S(1)}, u32[]{:S(2)}) copy-start(f32[96,256]{1,0:T(8,128)S(1)} %collective-permute-done.1.refs_2_) | copy-start | bytes 294916
  23.1 1.3 %collective-permute-start.6 = (f32[96,256]{1,0:T(8,128)S(1)}, f32[96,256]{1,0:T(8,128)S(1)}, u32[]{:S(2)}, u32[]{:S(2)}) collective-permute-start(f32[96,256]{1,0:T(8,128)S(1)} %collective-permute-done.2.refs_3_), channel_id=1, source_target_pairs={{0,1},{1,0},{2,3},{3,2},{4,5},{5,4},{6,7},{7,6},{8,9},{9,8},{10,11... | collective-permute-start | bytes 294920 | tf_op jit(solution)/shard_map/ppermute | solution.py:48
  23.4 1.4 %copy-start.17 = (f32[96,256]{1,0:T(8,128)}, f32[96,256]{1,0:T(8,128)S(1)}, u32[]{:S(2)}) copy-start(f32[96,256]{1,0:T(8,128)S(1)} %collective-permute-done.7.refs_8_) | copy-start | bytes 294916
  23.4 1.3 %collective-permute-start.5 = (f32[96,256]{1,0:T(8,128)S(1)}, f32[96,256]{1,0:T(8,128)S(1)}, u32[]{:S(2)}, u32[]{:S(2)}) collective-permute-start(f32[96,256]{1,0:T(8,128)S(1)} %collective-permute-done.1.refs_2_), channel_id=1, source_target_pairs={{0,1},{1,0},{2,3},{3,2},{4,5},{5,4},{6,7},{7,6},{8,9},{9,8},{10,11... | collective-permute-start | bytes 294920 | tf_op jit(solution)/shard_map/ppermute | solution.py:48
  24.4 0.6 copy-start.18
  25.0 0.6 copy-start.19
  30.3 20.8 %collective-permute-start.9 = (f32[256,384]{1,0:T(8,128)}, f32[256,384]{1,0:T(8,128)S(1)}, u32[]{:S(2)}, u32[]{:S(2)}) collective-permute-start(f32[256,384]{1,0:T(8,128)} %get-tuple-element.10), channel_id=1, source_target_pairs={{16,0},{32,16},{48,32},{64,48},{80,64},{96,80},{112,96},{128,112},... | collective-permute-start | bytes 1179656 | tf_op jit(solution)/shard_map/ppermute | solution.py:159
  38.8 9.8 %collective-permute-start.13 = (f32[144,256]{1,0:T(8,128)S(1)}, f32[144,256]{1,0:T(8,128)S(1)}, u32[]{:S(2)}, u32[]{:S(2)}) collective-permute-start(f32[144,256]{1,0:T(8,128)S(1)} %slice.18.refs_0_), channel_id=1, source_target_pairs={{0,12},{1,13},{2,14},{3,15},{4,8},{5,9},{6,10},{7,11},{8,4},{9,5},... | collective-permute-start | bytes 442376 | tf_op jit(solution)/shard_map/ppermute | solution.py:48
  42.3 8.8 %copy-start.6 = (f32[288,256]{1,0:T(8,128)}, f32[288,256]{1,0:T(8,128)S(1)}, u32[]{:S(2)}) copy-start(f32[288,256]{1,0:T(8,128)S(1)} %collective-permute-done.12.refs_4_) | copy-start | bytes 884740
  42.3 8.8 %collective-permute-start.16 = (f32[288,256]{1,0:T(8,128)S(1)}, f32[288,256]{1,0:T(8,128)S(1)}, u32[]{:S(2)}, u32[]{:S(2)}) collective-permute-start(f32[288,256]{1,0:T(8,128)S(1)} %collective-permute-done.12.refs_4_), channel_id=1, source_target_pairs={{0,1},{1,0},{2,3},{3,2},{4,5},{5,4},{6,7},{7,6},{8,9},{9,8},{10,11... | collective-permute-start | bytes 884744 | tf_op jit(solution)/shard_map/ppermute | solution.py:48
  42.3 8.8 %copy-start.7 = (f32[288,256]{1,0:T(8,128)}, f32[288,256]{1,0:T(8,128)S(1)}, u32[]{:S(2)}) copy-start(f32[288,256]{1,0:T(8,128)S(1)} %collective-permute-done.11.refs_3_) | copy-start | bytes 884740
  42.3 8.7 %collective-permute-start.15 = (f32[288,256]{1,0:T(8,128)S(1)}, f32[288,256]{1,0:T(8,128)S(1)}, u32[]{:S(2)}, u32[]{:S(2)}) collective-permute-start(f32[288,256]{1,0:T(8,128)S(1)} %collective-permute-done.11.refs_3_), channel_id=1, source_target_pairs={{0,1},{1,0},{2,3},{3,2},{4,5},{5,4},{6,7},{7,6},{8,9},{9,8},{10,11... | collective-permute-start | bytes 884744 | tf_op jit(solution)/shard_map/ppermute | solution.py:48
  42.8 8.3 %copy-start.8 = (f32[288,256]{1,0:T(8,128)}, f32[288,256]{1,0:T(8,128)S(1)}, u32[]{:S(2)}) copy-start(f32[288,256]{1,0:T(8,128)S(1)} %collective-permute-done.10.refs_2_) | copy-start | bytes 884740
  42.8 8.3 %collective-permute-start.14 = (f32[288,256]{1,0:T(8,128)S(1)}, f32[288,256]{1,0:T(8,128)S(1)}, u32[]{:S(2)}, u32[]{:S(2)}) collective-permute-start(f32[288,256]{1,0:T(8,128)S(1)} %collective-permute-done.10.refs_2_), channel_id=1, source_target_pairs={{0,1},{1,0},{2,3},{3,2},{4,5},{5,4},{6,7},{7,6},{8,9},{9,8},{10,11... | collective-permute-start | bytes 884744 | tf_op jit(solution)/shard_map/ppermute | solution.py:48
  48.6 2.5 %copy-start.12 = (f32[144,256]{1,0:T(8,128)}, f32[144,256]{1,0:T(8,128)S(1)}, u32[]{:S(2)}) copy-start(f32[144,256]{1,0:T(8,128)S(1)} %collective-permute-done.13.refs_5_) | copy-start | bytes 442372
  48.6 1.4 %collective-permute-start.17 = (f32[144,256]{1,0:T(8,128)S(1)}, f32[144,256]{1,0:T(8,128)S(1)}, u32[]{:S(2)}, u32[]{:S(2)}) collective-permute-start(f32[144,256]{1,0:T(8,128)S(1)} %collective-permute-done.13.refs_5_), channel_id=1, source_target_pairs={{0,1},{1,0},{2,3},{3,2},{4,5},{5,4},{6,7},{7,6},{8,9},{9,8},{10,11... | collective-permute-start | bytes 442376 | tf_op jit(solution)/shard_map/ppermute | solution.py:48
  50.0 1.2 %copy-start.13 = (f32[144,256]{1,0:T(8,128)}, f32[144,256]{1,0:T(8,128)S(1)}, u32[]{:S(2)}) copy-start(f32[144,256]{1,0:T(8,128)S(1)} %collective-permute-done.17.refs_9_) | copy-start | bytes 442372
  51.0 0.8 copy-start.5
  51.0 0.9 copy-start.9
  51.1 0.9 %copy-start.10 = (f32[288,256]{1,0:T(8,128)}, f32[288,256]{1,0:T(8,128)S(1)}, u32[]{:S(2)}) copy-start(f32[288,256]{1,0:T(8,128)S(1)} %collective-permute-done.15.refs_7_) | copy-start | bytes 884740
  51.1 1.0 %copy-start.11 = (f32[288,256]{1,0:T(8,128)}, f32[288,256]{1,0:T(8,128)S(1)}, u32[]{:S(2)}) copy-start(f32[288,256]{1,0:T(8,128)S(1)} %collective-permute-done.14.refs_6_) | copy-start | bytes 884740
  60.4 15.4 %collective-permute-start.18 = (f32[256,384]{1,0:T(8,128)}, f32[256,384]{1,0:T(8,128)S(1)}, u32[]{:S(2)}, u32[]{:S(2)}) collective-permute-start(f32[256,384]{1,0:T(8,128)} %get-tuple-element.11), channel_id=1, source_target_pairs={{0,16},{16,32},{32,48},{48,64},{64,80},{80,96},{96,112},{112,128},... | collective-permute-start | bytes 1179656 | tf_op jit(solution)/shard_map/ppermute | solution.py:159
  75.7 0.7 copy-start.2
